TPU v7x, 32 devices: a whole 2x2x4 slice. The times are simulated.
32 devices in a mesh: samp: 16 (over z, x, core), snp: 2 (over y).
Axes of the slice: x: 2, y: 2, z: 4, core: 2. Of those that a mesh axis runs over, the one named last changes fastest.
Arguments:
- genotypes: int32 [65536, 4096], P('samp', 'snp'), may hold values from 0 to 2, as said below
- allele_freq: float32 [4096], P('snp'), may hold values from 0.05 to 0.5
- snp_bins: int32 [4096], P('snp'), may hold values from 0 to 11, as said below
- probes: bfloat16 [64, 65536], P(None, 'samp'), may hold values from -6 to 6
- variances: float32 [13], replicated, may hold values from 0.1 to 1
Outputs:
- projected: float32 [65536, 768], P(('samp', 'snp'))
- combined: float32 [64, 65536], P(None, ('samp', 'snp'))
Inputs may be any that keep to these rules, and one draw needn't show every extreme that they name: `genotypes`: dosages 0, 1 or 2. `snp_bins`: every component has at least one SNP.
All inputs are finite; a program needn't handle non-finite values.
Results may differ from a plain program's by a relative error of at most 0.0065.
Values may be sent and summed in bfloat16 or wider, within the bound.
A program may use at most 192 MiB of HBM per device.

v0:
```python
import jax
import jax.numpy as jnp
from jax import lax
from jax.sharding import PartitionSpec as P

COMPONENTS = 12


def standardize(dosage_block, allele_freq):
    spread = jnp.sqrt(2.0 * allele_freq * (1.0 - allele_freq))
    return ((dosage_block.astype(jnp.float32) - 2.0 * allele_freq) / spread).astype(jnp.bfloat16)


def build_weights(scores, snp_bins, counts, labels):
    onehot = (snp_bins[:, None] == labels[None, :]).astype(jnp.float32)
    factor = jnp.sum(onehot * lax.rsqrt(counts)[None, :], 1)
    width = scores.shape[0]
    spread_out = (scores.T * factor[:, None])[:, None, :] * onehot[:, :, None]
    return spread_out.reshape(snp_bins.shape[0], labels.shape[0] * width).astype(jnp.bfloat16)


def body(genotypes, allele_freq, snp_bins, probes, variances):
    standard = standardize(genotypes, allele_freq)
    partial_scores = jnp.dot(probes, standard, preferred_element_type=jnp.float32)
    whole_rows = standard.shape[0] * lax.axis_size("samp")
    scores = lax.psum(partial_scores, "samp") / jnp.sqrt(jnp.float32(whole_rows))
    groups = lax.axis_size("snp")
    own_rows = standard.shape[0] // groups
    snp_index = lax.axis_index("snp")
    labels = jnp.arange(COMPONENTS, dtype=jnp.int32)
    sample_rows = lax.all_to_all(standard, "snp", split_axis=0, concat_axis=1, tiled=True)
    packed = jnp.concatenate([scores, snp_bins.astype(jnp.float32)[None, :]], 0)
    gathered = lax.all_gather(packed, "snp", axis=1, tiled=True)
    scores_full = gathered[:-1]
    bins_full = gathered[-1].astype(jnp.int32)
    all_hits = (bins_full[:, None] == labels[None, :]).astype(jnp.float32)
    counts = jnp.sum(all_hits, 0)
    weights = build_weights(scores_full, bins_full, counts, labels)
    projected = jnp.dot(sample_rows, weights, preferred_element_type=jnp.float32)
    width = probes.shape[0]
    stacked = projected.reshape(own_rows, COMPONENTS, width)
    own_probes = lax.dynamic_slice_in_dim(probes, snp_index * own_rows, own_rows, 1).astype(
        jnp.float32
    )
    combined = (
        jnp.einsum("nmb,m->bn", stacked, variances[:COMPONENTS])
        + variances[COMPONENTS] * own_probes
    )
    return (projected, combined)


def solution(mesh):
    placed = (P("samp", "snp"), P("snp"), P("snp"), P(None, "samp"), P())
    return jax.shard_map(
        body,
        mesh=mesh,
        in_specs=placed,
        out_specs=(P(("samp", "snp"), None), P(None, ("samp", "snp"))),
        check_vma=False,
    )
```

profile of v0, /device:TPU:0, one launch (start us, length us, event | category | flops | bytes accessed | tf_op | source)
XLA Modules:
  0.0 353.7 jit_solution(13495616757091779543)
XLA Ops:
  7.2 0.7 broadcast_multiply_fusion.1
  7.9 18.2 %divide_convert_fusion = bf16[4096,2048]{1,0:T(8,128)(2,1)} fusion(s32[4096,2048]{1,0:T(8,128)} %param.5, f32[2048]{0:T(1024)S(1)} %get-tuple-element.9, f32[2048]{0:T(1024)S(1)} %get-tuple-element.8), kind=kLoop, calls=%fused_computation | loop fusion | flops 33554432 | bytes 50348032 | tf_op jit(solution)/shard_map/convert_element_type | solution.py:11
  26.1 0.0 copy-start
  26.1 9.8 %all-to-all-start = ((bf16[2,2048,2048]{2,1,0:T(8,128)(2,1)}), bf16[2,2048,2048]{2,1,0:T(8,128)(2,1)}, u32[]{:S(2)}, u32[]{:S(2)}) async-start(bf16[2,2048,2048]{2,1,0:T(8,128)(2,1)} %bitcast.23), calls=%async_computation | async-start | bytes 33554432 | tf_op jit(solution)/shard_map/all_to_all | solution.py:31
  35.9 0.0 copy-start.1
  35.9 0.0 copy-start.2
  35.9 0.0 all-reduce.2.cloned.1.call-start
  36.0 0.0 copy-done
  36.0 9.6 %convolution_bitcast_fusion = f32[64,2048]{1,0:T(8,128)} fusion(bf16[64,4096]{1,0:T(8,128)(2,1)S(1)} %copy-done, bf16[4096,2048]{1,0:T(8,128)(2,1)} %divide_convert_fusion), kind=kOutput, calls=%fused_computation.4 | convolution fusion | flops 1073741824 | bytes 17825792 | tf_op jit(solution)/shard_map/dot_general | solution.py:24
  45.6 0.0 all-reduce.2.cloned.1.call-update
  45.6 0.2 all-gather.2.cloned.1.call-start
  45.8 0.0 copy-done.1
  45.8 93.9 %all-reduce.2.cloned.1.call-done = f32[64,2048]{1,0:T(8,128)} async-done(((f32[64,2048]{1,0:T(8,128)}), f32[64,2048]{1,0:T(8,128)}) %all-reduce.2.cloned.1.call-update) | async-done | bytes 524304 | tf_op jit(solution)/shard_map/psum | solution.py:26
  139.7 1.1 broadcast_multiply_fusion
  140.8 0.9 pad_maximum_fusion
  141.7 0.0 all-gather.2.cloned.1.call-update
  141.7 0.0 copy-done.2
  141.7 0.7 slice.15
  142.4 35.5 %all-gather.2.cloned.1.call-done = f32[65,4096]{1,0:T(8,128)} async-done(((f32[65,2048]{1,0:T(8,128)}), f32[65,4096]{1,0:T(8,128)}) %all-gather.2.cloned.1.call-update) | async-done | bytes 1064976 | tf_op jit(solution)/shard_map/all_gather | solution.py:33
  177.9 0.9 slice_convert_fusion
  178.8 0.2 fusion.4
  179.0 0.1 select_reduce_fusion
  179.1 1.3 fusion.2
  180.5 4.1 %multiply_convert_fusion = bf16[4096,12,64]{0,2,1:T(8,128)(2,1)} fusion(f32[4096,12]{0,1:T(8,128)S(1)} %fusion.3, f32[4096,64]{0,1:T(8,128)S(1)} %fusion.2), kind=kLoop, calls=%fused_computation.1 | loop fusion | flops 6291456 | bytes 7536640 | tf_op jit(solution)/shard_map/convert_element_type | solution.py:19
  184.6 47.7 %all-to-all-done = bf16[2,2048,2048]{2,1,0:T(8,128)(2,1)} async-done(((bf16[2,2048,2048]{2,1,0:T(8,128)(2,1)}), bf16[2,2048,2048]{2,1,0:T(8,128)(2,1)}, u32[]{:S(2)}, u32[]{:S(2)}) %all-to-all-start) | async-done | bytes 16777248 | tf_op jit(solution)/shard_map/all_to_all | solution.py:31
  232.3 22.4 %copy.10 = bf16[2048,2,2048]{0,2,1:T(8,128)(2,1)} copy(bf16[2048,2,2048]{2,0,1:T(8,128)(2,1)} %bitcast.1) | data formatting | bytes 33554432 | tf_op jit(solution)/shard_map/all_to_all | solution.py:31
  254.7 20.1 %fusion.7 = f32[2048,768]{0,1:T(8,128)} fusion(bf16[4096,768]{0,1:T(8,128)(2,1)} %bitcast.26, bf16[2048,4096]{0,1:T(8,128)(2,1)} %bitcast.25), kind=kOutput, calls=%fused_computation.19 | convolution fusion | flops 12884901888 | bytes 29360128 | tf_op jit(solution)/shard_map/dot_general | solution.py:39
  274.8 6.6 %copy.11 = f32[2048,768]{1,0:T(8,128)} copy(f32[2048,768]{0,1:T(8,128)} %fusion.7) | data formatting | bytes 12582912
  281.4 25.7 %fusion = f32[1,2048,64]{0,1,2:T(8,128)} fusion(f32[2048,12,64]{0,2,1:T(8,128)} %bitcast.24, f32[13]{0:T(128)S(1)} %copy-done.2), kind=kOutput, calls=%fused_computation.2 | convolution fusion | flops 3145728 | bytes 6815796 | tf_op jit(solution)/shard_map/nmb,m->bn/dot_general | solution.py:46
  307.0 38.3 %copy.13 = f32[1,2048,64]{1,2,0:T(8,128)S(1)} copy(f32[1,2048,64]{0,1,2:T(8,128)} %fusion) | data formatting | bytes 1048576 | tf_op jit(solution)/shard_map/nmb,m->bn/dot_general | solution.py:46
  345.3 1.6 bitcast_add_fusion
  (3 shorter events, 0.0 us)
Async XLA Ops:
  26.1 9.9 %copy-start = (bf16[64,4096]{1,0:T(8,128)(2,1)S(1)}, bf16[64,4096]{1,0:T(8,128)(2,1)}, u32[]{:S(2)}) copy-start(bf16[64,4096]{1,0:T(8,128)(2,1)} %param.8) | copy-start | bytes 1572868
  26.1 206.2 %all-to-all-start = ((bf16[2,2048,2048]{2,1,0:T(8,128)(2,1)}), bf16[2,2048,2048]{2,1,0:T(8,128)(2,1)}, u32[]{:S(2)}, u32[]{:S(2)}) async-start(bf16[2,2048,2048]{2,1,0:T(8,128)(2,1)} %bitcast.23), calls=%async_computation | async-start | bytes 33554432 | tf_op jit(solution)/shard_map/all_to_all | solution.py:31
  35.9 9.9 %copy-start.1 = (s32[2048]{0:T(1024)S(1)}, s32[2048]{0:T(1024)}, u32[]{:S(2)}) copy-start(s32[2048]{0:T(1024)} %param.7) | copy-start | bytes 24580
  35.9 105.8 %copy-start.2 = (f32[13]{0:T(128)S(1)}, f32[13]{0:T(128)}, u32[]{:S(2)}) copy-start(f32[13]{0:T(128)} %param.9) | copy-start | bytes 160
  35.9 103.8 %all-reduce.2.cloned.1.call-start = ((), (), s32[]{:S(2)}) async-start(), calls=%async_computation.1 | async-start | bytes 1048576 | tf_op jit(solution)/shard_map/psum | solution.py:26
  45.6 132.3 %all-gather.2.cloned.1.call-start = ((), (), s32[]{:S(2)}) async-start(), calls=%async_computation.2 | async-start | bytes 1769472 | tf_op jit(solution)/shard_map/all_gather | solution.py:33
Sparse Core Ops, SparseCore 0:
  45.7 93.9 all-reduce.1
  141.8 35.9 all-gather.1
where the time goes:
time: 355 us; the launch traced here: 354 us
  waiting for transfers between devices  177 us (50%)
  local copies, waits for them, and re-layouts  67.9 us (19%)
  matrix products  55.4 us (16%)
  other arithmetic  29.1 us (8%)
  between operations  14.1 us (4%)
  starting transfers between devices  10.1 us (3%)
    psum x1, waiting for transfers between devices, body(): lax.psum(partial_scores, 'samp') / jnp.sqrt(jnp.float32(whole_rows))  93.9 us
    all_to_all x1, waiting for transfers between devices, body(): lax.all_to_all(standard, 'snp', split_axis=0, concat_axis=1, tiled=True)  47.7 us
    dot_general x1, local copies, waits for them, and re-layouts, body(): jnp.einsum('nmb,m->bn', stacked, variances[:COMPONENTS])  38.3 us
    all_gather x1, waiting for transfers between devices, body(): gathered = lax.all_gather(packed, 'snp', axis=1, tiled=True)  35.5 us
    dot_general x1, matrix products, body(): jnp.einsum('nmb,m->bn', stacked, variances[:COMPONENTS])  25.7 us
    all_to_all x1, local copies, waits for them, and re-layouts, body(): lax.all_to_all(standard, 'snp', split_axis=0, concat_axis=1, tiled=True)  22.4 us
    dot_general x1, matrix products, body(): jnp.dot(sample_rows, weights, preferred_element_type=jnp.float32)  20.1 us
    convert_element_type x1, other arithmetic, standardize(): ((dosage_block.astype(jnp.float32) - 2.0 * allele_freq) / spread).astype(...  18.2 us
  transfers between devices with their start and end apart: 3, of which 3 were waited for; matrix products, arithmetic and copies ran while one was open for 5% of the time, Pallas kernels for 0%

commit v1 on v0

v1 whole, which is shorter than its diff:
```python
import jax
import jax.numpy as jnp
from jax import lax
from jax.sharding import PartitionSpec as P

COMPONENTS = 12
CHUNKS = 4


def standardize(dosage_block, allele_freq):
    spread = jnp.sqrt(2.0 * allele_freq * (1.0 - allele_freq))
    return ((dosage_block.astype(jnp.float32) - 2.0 * allele_freq) / spread).astype(jnp.bfloat16)


def body(genotypes, allele_freq, snp_bins, probes, variances):
    groups = lax.axis_size("snp")
    me = lax.axis_index("snp")
    labels = jnp.arange(COMPONENTS, dtype=jnp.int32)
    onehot = (snp_bins[:, None] == labels[None, :]).astype(jnp.float32)
    counts = lax.psum(jnp.sum(onehot, 0), "snp")
    standard = standardize(genotypes, allele_freq)
    partial_scores = jnp.dot(probes, standard, preferred_element_type=jnp.float32)
    whole_rows = standard.shape[0] * lax.axis_size("samp")
    scores = lax.psum(partial_scores, "samp") / jnp.sqrt(jnp.float32(whole_rows))
    factor = jnp.sum(onehot * lax.rsqrt(counts)[None, :], 1)
    width = scores.shape[0]
    weights = ((scores.T * factor[:, None])[:, None, :] * onehot[:, :, None]).reshape(
        snp_bins.shape[0], COMPONENTS * width
    ).astype(jnp.bfloat16)
    own_rows = standard.shape[0] // groups
    piece = own_rows // CHUNKS

    def product(target, chunk):
        rows = lax.dynamic_slice_in_dim(standard, target * own_rows + chunk * piece, piece, 0)
        return jnp.dot(rows, weights, preferred_element_type=jnp.float32)

    got = [[] for _ in range(CHUNKS)]
    for shift in range(1, groups):
        ring = [(i, (i + shift) % groups) for i in range(groups)]
        for chunk in range(CHUNKS):
            sent = product(lax.rem(me + shift, groups), chunk).astype(jnp.bfloat16)
            got[chunk].append(lax.ppermute(sent, "snp", ring))
    blocks = []
    for chunk in range(CHUNKS):
        total = product(me, chunk)
        for term in got[chunk]:
            total = total + term.astype(jnp.float32)
        blocks.append(total)
    projected = jnp.concatenate(blocks, 0)
    stacked = projected.reshape(own_rows, COMPONENTS, width)
    own_probes = lax.dynamic_slice_in_dim(probes, me * own_rows, own_rows, 1).astype(jnp.float32)
    combined = (
        jnp.einsum("nmb,m->bn", stacked, variances[:COMPONENTS])
        + variances[COMPONENTS] * own_probes
    )
    return (projected, combined)


def solution(mesh):
    placed = (P("samp", "snp"), P("snp"), P("snp"), P(None, "samp"), P())
    return jax.shard_map(
        body,
        mesh=mesh,
        in_specs=placed,
        out_specs=(P(("samp", "snp"), None), P(None, ("samp", "snp"))),
        check_vma=False,
    )
```

time: 355 us -> 280 us (0.79)
  waiting for transfers between devices: 177 us -> 139 us
  local copies, waits for them, and re-layouts: 67.9 us -> 48.6 us
  matrix products: 55.4 us -> 45.5 us
  other arithmetic: 29.1 us -> 20.2 us
  blocking collectives: 0 us -> 6.08 us
  starting transfers between devices: 10.1 us -> 4.81 us
    ppermute x0 -> x4, waiting for transfers between devices: none -> 52.8 us  [body(): got[chunk].append(lax.ppermute(sent, 'snp', ring))]
    all_to_all x1 -> x0, waiting for transfers between devices: 47.7 us -> none  [body(): lax.all_to_all(standard, 'snp', split_axis=0, concat_axis=1, tiled=True)]
    all_gather x1 -> x0, waiting for transfers between devices: 35.5 us -> none  [body(): gathered = lax.all_gather(packed, 'snp', axis=1, tiled=True)]
    all_to_all x1 -> x0, local copies, waits for them, and re-layouts: 22.4 us -> none  [body(): lax.all_to_all(standard, 'snp', split_axis=0, concat_axis=1, tiled=True)]
    all_to_all x1 -> x0, starting transfers between devices: 9.81 us -> none  [body(): lax.all_to_all(standard, 'snp', split_axis=0, concat_axis=1, tiled=True)]
    psum x1, waiting for transfers between devices: 93.9 us -> 86.6 us  [body(): lax.psum(partial_scores, 'samp') / jnp.sqrt(jnp.float32(whole_rows))]
    psum x0 -> x1, blocking collectives: none -> 6.08 us  [body(): counts = lax.psum(jnp.sum(onehot, 0), 'snp')]
    dot_general x1, matrix products: 9.58 us -> 3.86 us  [body(): jnp.dot(probes, standard, preferred_element_type=jnp.float32)]
  transfers between devices with their start and end apart: 3 -> 5, of which waited for: 3 -> 5; matrix products, arithmetic and copies ran while one was open for 5% -> 5% of each run, Pallas kernels for 0% -> 0%
where the time goes in v1:
time: 280 us; the launch traced here: 279 us
  waiting for transfers between devices  139 us (50%)
  local copies, waits for them, and re-layouts  48.6 us (17%)
  matrix products  45.5 us (16%)
  other arithmetic  20.2 us (7%)
  between operations  14.2 us (5%)
  blocking collectives  6.08 us (2%)
  starting transfers between devices  4.81 us (2%)
    psum x1, waiting for transfers between devices, body(): lax.psum(partial_scores, 'samp') / jnp.sqrt(jnp.float32(whole_rows))  86.6 us
    ppermute x4, waiting for transfers between devices, body(): got[chunk].append(lax.ppermute(sent, 'snp', ring))  52.8 us
    dot_general x1, local copies, waits for them, and re-layouts, body(): jnp.einsum('nmb,m->bn', stacked, variances[:COMPONENTS])  38.3 us
    dot_general x1, matrix products, body(): jnp.einsum('nmb,m->bn', stacked, variances[:COMPONENTS])  23.2 us
    dot_general x8, matrix products, product(): return jnp.dot(rows, weights, preferred_element_type=jnp.float32)  18.4 us
    convert_element_type x1, other arithmetic, standardize(): ((dosage_block.astype(jnp.float32) - 2.0 * allele_freq) / spread).astype(...  13 us
    psum x1, blocking collectives, body(): counts = lax.psum(jnp.sum(onehot, 0), 'snp')  6.08 us
    unnamed x12, local copies, waits for them, and re-layouts  5.74 us
  transfers between devices with their start and end apart: 5, of which 5 were waited for; matrix products, arithmetic and copies ran while one was open for 5% of the time, Pallas kernels for 0%

profile of v1, /device:TPU:0, one launch (start us, length us, event | category | flops | bytes accessed | tf_op | source)
XLA Modules:
  0.0 278.8 jit_solution(911292419012415044)
XLA Ops:
  7.2 0.0 all-reduce.2.cloned.1.call-start
  7.2 0.7 broadcast_multiply_fusion.1
  7.9 0.0 copy-start.2
  7.9 13.0 %divide_convert_fusion = bf16[4096,2048]{1,0:T(8,128)(2,1)S(1)} fusion(s32[4096,2048]{1,0:T(8,128)} %param.5, f32[2048]{0:T(1024)S(1)} %get-tuple-element.3, f32[2048]{0:T(1024)S(1)} %get-tuple-element.2), kind=kLoop, calls=%fused_computation | loop fusion | flops 33554432 | bytes 50348032 | tf_op jit(solution)/shard_map/convert_element_type | solution.py:12
  20.9 0.0 copy-start
  21.0 5.7 %copy-done = bf16[4096,2048]{1,0:T(8,128)(2,1)} copy-done((bf16[4096,2048]{1,0:T(8,128)(2,1)}, bf16[4096,2048]{1,0:T(8,128)(2,1)S(1)}, u32[]{:S(2)}) %copy-start) | copy-done | bytes 16777240
  26.7 0.0 copy-done.2
  26.7 0.0 copy-start.4
  26.7 0.0 copy-start.5
  26.7 3.9 %convolution_bitcast_fusion = f32[64,2048]{1,0:T(8,128)} fusion(bf16[64,4096]{1,0:T(8,128)(2,1)S(1)} %copy-done.2, bf16[4096,2048]{1,0:T(8,128)(2,1)S(1)} %divide_convert_fusion), kind=kOutput, calls=%fused_computation.5 | convolution fusion | flops 1073741824 | bytes 17825792 | tf_op jit(solution)/shard_map/dot_general | solution.py:22
  30.5 0.0 all-reduce.2.cloned.1.call-update
  30.6 0.0 copy-done.4
  30.6 0.1 fusion.31
  30.7 6.1 %psum.15 = f32[12]{0:T(128)S(1)} all-reduce(f32[12]{0:T(128)S(1)} %fusion.31), channel_id=1, replica_groups=mesh['samp'=16,'snp'=2] {'snp'}, use_global_device_ids=true, to_apply=%region_2.0 | all-reduce | flops 12 | bytes 96 | tf_op jit(solution)/shard_map/psum | solution.py:20
  36.8 0.1 select_reduce_fusion
  36.9 0.0 copy-done.5
  36.9 0.6 slice.7
  37.5 86.6 %all-reduce.2.cloned.1.call-done = f32[64,2048]{1,0:T(8,128)} async-done(((f32[64,2048]{1,0:T(8,128)}), f32[64,2048]{1,0:T(8,128)}) %all-reduce.2.cloned.1.call-update) | async-done | bytes 524304 | tf_op jit(solution)/shard_map/psum | solution.py:24
  124.1 1.1 multiply_bitcast_fusion
  125.2 0.7 multiply_convert_fusion
  125.9 0.0 copy-start.1
  125.9 3.6 %fusion.18 = bf16[512,768]{1,0:T(8,128)(2,1)S(1)} fusion(bf16[2048,768]{0,1:T(8,128)(2,1)S(1)} %bitcast.25, bf16[4096,2048]{1,0:T(8,128)(2,1)} %copy-done, s32[]{:T(128)S(6)} %select_n.26), kind=kOutput, calls=%fused_computation.26 | convolution fusion | flops 1611005952 | bytes 6029316 | tf_op jit(solution)/shard_map/dot_general | solution.py:35
  129.5 1.5 collective-permute-start
  131.0 3.7 %fusion.21 = bf16[512,768]{1,0:T(8,128)(2,1)S(1)} fusion(bf16[2048,768]{0,1:T(8,128)(2,1)S(1)} %bitcast.26, bf16[4096,2048]{1,0:T(8,128)(2,1)} %copy-done, s32[]{:T(128)S(6)} %select_n.28), kind=kOutput, calls=%fused_computation.27 | convolution fusion | flops 1611005952 | bytes 6029316 | tf_op jit(solution)/shard_map/dot_general | solution.py:35
  134.8 1.1 collective-permute-start.1
  135.8 0.0 copy-done.1
  135.9 1.8 fusion.24
  137.7 1.1 collective-permute-start.2
  138.7 1.8 fusion.27
  140.6 1.1 collective-permute-start.3
  141.7 8.3 %collective-permute-done = bf16[512,768]{1,0:T(8,128)(2,1)S(1)} collective-permute-done((bf16[512,768]{1,0:T(8,128)(2,1)S(1)}, bf16[512,768]{1,0:T(8,128)(2,1)S(1)}, u32[]{:S(2)}, u32[]{:S(2)}) %collective-permute-start) | collective-permute-done | bytes 786464 | tf_op jit(solution)/shard_map/ppermute | solution.py:42
  150.0 1.8 convert_add_fusion.3
  151.8 15.0 %collective-permute-done.1 = bf16[512,768]{1,0:T(8,128)(2,1)S(1)} collective-permute-done((bf16[512,768]{1,0:T(8,128)(2,1)S(1)}, bf16[512,768]{1,0:T(8,128)(2,1)S(1)}, u32[]{:S(2)}, u32[]{:S(2)}) %collective-permute-start.1) | collective-permute-done | bytes 786464 | tf_op jit(solution)/shard_map/ppermute | solution.py:42
  166.9 1.8 convert_add_fusion.2
  168.7 15.0 %collective-permute-done.2 = bf16[512,768]{1,0:T(8,128)(2,1)S(1)} collective-permute-done((bf16[512,768]{1,0:T(8,128)(2,1)S(1)}, bf16[512,768]{1,0:T(8,128)(2,1)S(1)}, u32[]{:S(2)}, u32[]{:S(2)}) %collective-permute-start.2) | collective-permute-done | bytes 786464 | tf_op jit(solution)/shard_map/ppermute | solution.py:42
  183.7 1.8 convert_add_fusion.1
  185.5 14.4 %collective-permute-done.3 = bf16[512,768]{1,0:T(8,128)(2,1)S(1)} collective-permute-done((bf16[512,768]{1,0:T(8,128)(2,1)S(1)}, bf16[512,768]{1,0:T(8,128)(2,1)S(1)}, u32[]{:S(2)}, u32[]{:S(2)}) %collective-permute-start.3) | collective-permute-done | bytes 786464 | tf_op jit(solution)/shard_map/ppermute | solution.py:42
  200.0 2.1 convert_add_fusion
  202.0 2.9 %pad_maximum_fusion = f32[2048,768]{1,0:T(8,128)} fusion(f32[512,768]{1,0:T(8,128)S(1)} %convert_add_fusion, f32[512,768]{1,0:T(8,128)S(1)} %convert_add_fusion.1, f32[512,768]{1,0:T(8,128)S(1)} %convert_add_fusion.2, f32[512,768]{1,0:T(8,128)S(1)} %convert_add_fusion.3), kind=kLoop, calls=%fused_computation.3 | loop fusion | flops 4718592 | bytes 12582912 | tf_op jit(solution)/shard_map/concatenate | solution.py:49
  205.0 4.0 %copy.8 = bf16[2048,768]{0,1:T(8,128)(2,1)S(1)} copy(f32[2048,768]{1,0:T(8,128)} %pad_maximum_fusion) | data formatting | bytes 9437184 | tf_op jit(solution)/shard_map/concatenate | solution.py:49
  209.0 23.2 %fusion = f32[1,2048,64]{0,1,2:T(8,128)} fusion(bf16[2048,12,64]{0,2,1:T(8,128)(2,1)S(1)} %bitcast.24, f32[13]{0:T(128)S(1)} %copy-done.5), kind=kOutput, calls=%fused_computation.1 | convolution fusion | flops 3145728 | bytes 3670068 | tf_op jit(solution)/shard_map/nmb,m->bn/dot_general | solution.py:53
  232.1 0.0 copy-start.3
  232.1 38.3 %copy.10 = f32[1,2048,64]{1,2,0:T(8,128)S(1)} copy(f32[1,2048,64]{0,1,2:T(8,128)} %fusion) | data formatting | bytes 1048576 | tf_op jit(solution)/shard_map/nmb,m->bn/dot_general | solution.py:53
  270.4 0.0 copy-done.3
  270.5 1.5 bitcast_add_fusion
  (3 shorter events, 0.0 us)
Async XLA Ops:
  7.2 117.0 %all-reduce.2.cloned.1.call-start = ((), (), s32[]{:S(2)}) async-start(), calls=%async_computation | async-start | bytes 1048576 | tf_op jit(solution)/shard_map/psum | solution.py:24
  7.9 18.8 %copy-start.2 = (bf16[64,4096]{1,0:T(8,128)(2,1)S(1)}, bf16[64,4096]{1,0:T(8,128)(2,1)}, u32[]{:S(2)}) copy-start(bf16[64,4096]{1,0:T(8,128)(2,1)} %param.8) | copy-start | bytes 1572868
  20.9 5.7 %copy-start = (bf16[4096,2048]{1,0:T(8,128)(2,1)}, bf16[4096,2048]{1,0:T(8,128)(2,1)S(1)}, u32[]{:S(2)}) copy-start(bf16[4096,2048]{1,0:T(8,128)(2,1)S(1)} %divide_convert_fusion) | copy-start | bytes 50331652
  26.7 3.9 %copy-start.4 = (s32[2048]{0:T(1024)S(1)}, s32[2048]{0:T(1024)}, u32[]{:S(2)}) copy-start(s32[2048]{0:T(1024)} %param.7) | copy-start | bytes 24580
  26.7 10.3 %copy-start.5 = (f32[13]{0:T(128)S(1)}, f32[13]{0:T(128)}, u32[]{:S(2)}) copy-start(f32[13]{0:T(128)} %param.9) | copy-start | bytes 160
  125.9 9.9 %copy-start.1 = (bf16[4096,2048]{1,0:T(8,128)(2,1)S(1)}, bf16[4096,2048]{1,0:T(8,128)(2,1)}, u32[]{:S(2)}) copy-start(bf16[4096,2048]{1,0:T(8,128)(2,1)} %copy-done) | copy-start | bytes 50331652
  129.5 20.5 %collective-permute-start = (bf16[512,768]{1,0:T(8,128)(2,1)S(1)}, bf16[512,768]{1,0:T(8,128)(2,1)S(1)}, u32[]{:S(2)}, u32[]{:S(2)}) collective-permute-start(bf16[512,768]{1,0:T(8,128)(2,1)S(1)} %fusion.18), channel_id=1, source_target_pairs={{0,1},{1,0},{2,3},{3,2},{4,5},{5,4},{6,7},{7,6},{8,9},{9,8},{10,11... | collective-permute-start | bytes 2359304 | tf_op jit(solution)/shard_map/ppermute | solution.py:42
  134.8 32.1 %collective-permute-start.1 = (bf16[512,768]{1,0:T(8,128)(2,1)S(1)}, bf16[512,768]{1,0:T(8,128)(2,1)S(1)}, u32[]{:S(2)}, u32[]{:S(2)}) collective-permute-start(bf16[512,768]{1,0:T(8,128)(2,1)S(1)} %fusion.21), channel_id=1, source_target_pairs={{0,1},{1,0},{2,3},{3,2},{4,5},{5,4},{6,7},{7,6},{8,9},{9,8},{10,11... | collective-permute-start | bytes 2359304 | tf_op jit(solution)/shard_map/ppermute | solution.py:42
  137.7 46.0 %collective-permute-start.2 = (bf16[512,768]{1,0:T(8,128)(2,1)S(1)}, bf16[512,768]{1,0:T(8,128)(2,1)S(1)}, u32[]{:S(2)}, u32[]{:S(2)}) collective-permute-start(bf16[512,768]{1,0:T(8,128)(2,1)S(1)} %fusion.24), channel_id=1, source_target_pairs={{0,1},{1,0},{2,3},{3,2},{4,5},{5,4},{6,7},{7,6},{8,9},{9,8},{10,11... | collective-permute-start | bytes 2359304 | tf_op jit(solution)/shard_map/ppermute | solution.py:42
  140.6 59.4 %collective-permute-start.3 = (bf16[512,768]{1,0:T(8,128)(2,1)S(1)}, bf16[512,768]{1,0:T(8,128)(2,1)S(1)}, u32[]{:S(2)}, u32[]{:S(2)}) collective-permute-start(bf16[512,768]{1,0:T(8,128)(2,1)S(1)} %fusion.27), channel_id=1, source_target_pairs={{0,1},{1,0},{2,3},{3,2},{4,5},{5,4},{6,7},{7,6},{8,9},{9,8},{10,11... | collective-permute-start | bytes 2359304 | tf_op jit(solution)/shard_map/ppermute | solution.py:42
  232.1 38.3 %copy-start.3 = (bf16[64,4096]{1,0:T(8,128)(2,1)S(1)}, bf16[64,4096]{1,0:T(8,128)(2,1)}, u32[]{:S(2)}) copy-start(bf16[64,4096]{1,0:T(8,128)(2,1)} %param.8) | copy-start | bytes 1572868
Sparse Core Ops, SparseCore 0:
  30.7 93.4 all-reduce.1

commit v2 on v0

v2 whole, which is shorter than its diff:
```python
import functools

import jax
import jax.numpy as jnp
from jax import lax
from jax.experimental import pallas as pl
from jax.experimental.pallas import tpu as pltpu
from jax.sharding import PartitionSpec as P

COMPONENTS = 12
LABELS = 16
LANES = 128
TILE_BYTES = 2 << 20
DEPTH = 3
MESH = pl.DeviceIdType.MESH
F32 = jnp.float32
BF16 = jnp.bfloat16


class Plan:
    def __init__(self, rows, snps, width, samp, snp):
        self.rows, self.snps, self.width = rows, snps, width
        self.samp, self.snp = samp, snp
        self.total = COMPONENTS * width
        self.parts = 1
        for parts in (2,):
            span = snps // parts
            if span % LANES == 0 and width // (samp // min(samp, span // LANES)) >= 16:
                self.parts = parts
        self.span = snps // self.parts
        self.across = min(samp, self.span // LANES)
        self.down = samp // self.across
        self.high = width // self.down
        self.wide = self.span // self.across
        self.tile = min(rows, TILE_BYTES // (4 * self.span))
        self.tiles = rows // self.tile
        self.own = rows // snp
        self.chunk = min(256, self.own)
        self.chunks = self.own // self.chunk


def kernel(
    plan, geno, freq, bins, probes, lane_vars, noise_var, out, comb,
    dosages, standard, acc, rs_send, rs_recv, gathered, counts, factor, weights,
    part_send, part_recv, own, comb_rows,
    in_sem, rs_ssem, rs_rsem, ag_ssem, ag_rsem, ct_ssem, ct_rsem, ex_ssem, ex_rsem, out_sem, comb_sem,
):
    p = plan
    n, groups = p.samp, p.snp
    me, mine = lax.axis_index("samp"), lax.axis_index("snp")

    def fetch(step):
        part, tile, slot = step // p.tiles, step % p.tiles, step % DEPTH
        return pltpu.make_async_copy(
            geno.at[pl.ds(tile * p.tile, p.tile), pl.ds(pl.multiple_of(part * p.span, LANES), p.span)],
            dosages.at[slot],
            in_sem.at[slot],
        )

    steps = p.parts * p.tiles
    for step in range(min(DEPTH - 1, steps)):
        fetch(step).start()

    barrier = pltpu.get_barrier_semaphore()

    @pl.loop(1, n)
    def _(shift):
        pl.semaphore_signal(
            barrier, inc=1, device_id={"samp": (me + shift) % n, "snp": mine}, device_id_type=MESH
        )

    @pl.loop(1, groups)
    def _(shift):
        pl.semaphore_signal(
            barrier, inc=1, device_id={"samp": me, "snp": (mine + shift) % groups}, device_id_type=MESH
        )

    labels = lax.broadcasted_iota(jnp.int32, (LABELS, p.snps), 0)
    hits = labels == bins[...]
    counted = jnp.sum(hits.astype(F32), axis=1, keepdims=True)
    counts[0] = jnp.broadcast_to(counted, (LABELS, LANES))
    acc[...] = jnp.zeros_like(acc)
    pl.semaphore_wait(barrier, n - 1 + groups - 1)

    def count_copy(shift):
        return pltpu.make_async_remote_copy(
            src_ref=counts.at[0], dst_ref=counts.at[shift],
            send_sem=ct_ssem.at[shift - 1], recv_sem=ct_rsem.at[shift - 1],
            device_id={"samp": me, "snp": (mine + shift) % groups}, device_id_type=MESH,
        )

    for shift in range(1, groups):
        count_copy(shift).start()

    def scatter_copy(part, shift):
        peer = (me + shift) % n
        return pltpu.make_async_remote_copy(
            src_ref=rs_send.at[part, peer], dst_ref=rs_recv.at[part, shift - 1],
            send_sem=rs_ssem.at[part, shift - 1], recv_sem=rs_rsem.at[part, shift - 1],
            device_id={"samp": peer, "snp": mine}, device_id_type=MESH,
        )

    def gather_copy(part, shift):
        return pltpu.make_async_remote_copy(
            src_ref=gathered.at[part, me], dst_ref=gathered.at[part, me],
            send_sem=ag_ssem.at[part, shift - 1], recv_sem=ag_rsem.at[part, shift - 1],
            device_id={"samp": (me + shift) % n, "snp": mine}, device_id_type=MESH,
        )

    def arrival(part, shift):
        source = (me + n - shift) % n
        return pltpu.make_async_remote_copy(
            src_ref=gathered.at[part, source], dst_ref=gathered.at[part, source],
            send_sem=ag_ssem.at[part, shift - 1], recv_sem=ag_rsem.at[part, shift - 1],
            device_id={"samp": source, "snp": mine}, device_id_type=MESH,
        )

    def read_part(part):
        columns = slice(part * p.span, (part + 1) * p.span)
        allele = freq[:, columns]
        center = 2.0 * allele
        scale = 1.0 / jnp.sqrt(center * (1.0 - allele))

        @pl.loop(0, p.tiles)
        def _(tile):
            step = part * p.tiles + tile

            @pl.when(step + DEPTH - 1 < steps)
            def _():
                fetch(step + DEPTH - 1).start()

            fetch(step).wait()
            rows = pl.ds(pl.multiple_of(tile * p.tile, p.tile), p.tile)
            value = ((dosages[step % DEPTH].astype(F32) - center) * scale).astype(BF16)
            standard[rows, columns] = value
            acc[:, columns] += jnp.dot(probes[:, rows], value, preferred_element_type=F32)

        for piece in range(n):
            top, left = (piece // p.across) * p.high, part * p.span + (piece % p.across) * p.wide
            rs_send[part, piece] = acc[top : top + p.high, left : left + p.wide].astype(BF16)

        @pl.loop(1, n)
        def _(shift):
            scatter_copy(part, shift).start()

    def reduce_part(part):
        def add(shift, total):
            scatter_copy(part, shift).wait_recv()
            return total + rs_recv[part, shift - 1].astype(F32)

        total = lax.fori_loop(1, n, add, rs_send[part, me].astype(F32))
        left = pl.multiple_of(part * p.span + (me % p.across) * p.wide, LANES)
        whole_rows = jnp.float32(p.rows * n)
        scores = total / jnp.sqrt(whole_rows)
        gathered[part, me] = (scores * factor[0:1, pl.ds(left, p.wide)]).astype(BF16)

        @pl.loop(1, n)
        def _(shift):
            gather_copy(part, shift).start()

    def spread_part(part):
        @pl.loop(1, n)
        def _(shift):
            arrival(part, shift).wait_recv()

        repeat = LANES // p.width
        for column in range(p.across):
            left = part * p.span + column * p.wide
            pieces = [gathered[part, column + p.across * row].astype(F32) for row in range(p.down)]
            block = jnp.concatenate(pieces * repeat, axis=0)
            turned = block.T
            marks = jnp.broadcast_to(bins[:, left : left + p.wide].astype(F32), (LANES, p.wide)).T
            lane = lax.broadcasted_iota(jnp.int32, (p.wide, LANES), 1) // p.width
            for pair in range(p.total // LANES):
                label = (lane + pair * repeat).astype(F32)
                weights[left : left + p.wide, pair * LANES : (pair + 1) * LANES] = jnp.where(
                    marks == label, turned, 0.0
                ).astype(BF16)

    read_part(0)
    for shift in range(1, groups):
        count_copy(shift).wait_recv()
    whole = counts[0]
    for shift in range(1, groups):
        whole = whole + counts[shift]
    root = lax.rsqrt(whole[:, 0:1])
    row = jnp.sum(jnp.where(hits, root, 0.0), axis=0, keepdims=True)
    factor[...] = jnp.broadcast_to(row, factor.shape)
    for part in range(1, p.parts):
        read_part(part)
        reduce_part(part - 1)
    reduce_part(p.parts - 1)
    for part in range(p.parts):
        spread_part(part)

    def part_copy(index):
        shift, chunk = index // p.chunks, index % p.chunks
        rows = pl.ds(pl.multiple_of(chunk * p.chunk, p.chunk), p.chunk)
        return pltpu.make_async_remote_copy(
            src_ref=part_send.at[shift, rows], dst_ref=part_recv.at[shift, rows],
            send_sem=ex_ssem.at[index], recv_sem=ex_rsem.at[index],
            device_id={"samp": me, "snp": (mine + shift + 1) % groups}, device_id_type=MESH,
        )

    sends = (groups - 1) * p.chunks

    @pl.loop(0, sends)
    def _(index):
        shift, chunk = index // p.chunks, index % p.chunks
        target = (mine + shift + 1) % groups
        rows = pl.ds(pl.multiple_of(target * p.own + chunk * p.chunk, p.chunk), p.chunk)
        product = jnp.dot(standard[rows, :], weights[...], preferred_element_type=F32)
        part_send[shift, pl.ds(pl.multiple_of(chunk * p.chunk, p.chunk), p.chunk), :] = product.astype(BF16)
        part_copy(index).start()

    @pl.loop(0, p.chunks)
    def _(chunk):
        rows = pl.ds(pl.multiple_of(mine * p.own + chunk * p.chunk, p.chunk), p.chunk)
        here = pl.ds(pl.multiple_of(chunk * p.chunk, p.chunk), p.chunk)
        own[here, :] = jnp.dot(standard[rows, :], weights[...], preferred_element_type=F32)

    def out_copy(chunk):
        here = pl.ds(pl.multiple_of(chunk * p.chunk, p.chunk), p.chunk)
        return pltpu.make_async_copy(own.at[here], out.at[here], out_sem.at[chunk])

    def comb_copy(chunk):
        here = pl.ds(pl.multiple_of(chunk * p.chunk, p.chunk), p.chunk)
        return pltpu.make_async_copy(comb_rows.at[chunk], comb.at[:, here], comb_sem.at[chunk])

    @pl.loop(0, p.chunks)
    def _(chunk):
        here = pl.ds(pl.multiple_of(chunk * p.chunk, p.chunk), p.chunk)
        total = own[here, :]
        for shift in range(groups - 1):
            part_copy(shift * p.chunks + chunk).wait_recv()
            total = total + part_recv[shift, here, :].astype(F32)
        own[here, :] = total
        out_copy(chunk).start()
        folded = jnp.zeros((p.chunk, LANES), F32)
        for pair in range(p.total // LANES):
            lanes = slice(pair * LANES, (pair + 1) * LANES)
            folded = folded + total[:, lanes] * lane_vars[:, lanes]
        turned = folded.T
        mixed = turned[0 : p.width]
        for again in range(1, LANES // p.width):
            mixed = mixed + turned[again * p.width : (again + 1) * p.width]
        cols = pl.ds(pl.multiple_of(mine * p.own + chunk * p.chunk, p.chunk), p.chunk)
        comb_rows[chunk] = mixed + noise_var[:, 0:1] * probes[:, cols].astype(F32)
        comb_copy(chunk).start()

    @pl.loop(0, sends)
    def _(index):
        part_copy(index).wait_send()

    for part in range(p.parts):

        @pl.loop(1, n)
        def _(shift):
            scatter_copy(part, shift).wait_send()
            gather_copy(part, shift).wait_send()

    for shift in range(1, groups):
        count_copy(shift).wait_send()

    @pl.loop(0, p.chunks)
    def _(chunk):
        out_copy(chunk).wait()
        comb_copy(chunk).wait()


def body(genotypes, allele_freq, snp_bins, probes, variances):
    rows, snps = genotypes.shape
    width = probes.shape[0]
    p = Plan(rows, snps, width, lax.axis_size("samp"), lax.axis_size("snp"))
    n, groups = p.samp, p.snp
    lane_vars = jnp.repeat(variances[:COMPONENTS], width)[None, :]
    noise_var = jnp.broadcast_to(variances[COMPONENTS], (1, LANES))
    vmem, hbm = pl.BlockSpec(memory_space=pltpu.VMEM), pl.BlockSpec(memory_space=pl.ANY)
    dma = pltpu.SemaphoreType.DMA
    sends = (groups - 1) * p.chunks
    return pl.pallas_call(
        functools.partial(kernel, p),
        out_shape=(
            jax.ShapeDtypeStruct((p.own, p.total), F32),
            jax.ShapeDtypeStruct((width, p.own), F32),
        ),
        in_specs=[hbm, vmem, vmem, vmem, vmem, vmem],
        out_specs=(hbm, hbm),
        scratch_shapes=[
            pltpu.VMEM((DEPTH, p.tile, p.span), jnp.int32),
            pltpu.VMEM((rows, snps), BF16),
            pltpu.VMEM((width, snps), F32),
            pltpu.VMEM((p.parts, n, p.high, p.wide), BF16),
            pltpu.VMEM((p.parts, n - 1, p.high, p.wide), BF16),
            pltpu.VMEM((p.parts, n, p.high, p.wide), BF16),
            pltpu.VMEM((groups, LABELS, LANES), F32),
            pltpu.VMEM((8, snps), F32),
            pltpu.VMEM((snps, p.total), BF16),
            pltpu.VMEM((groups - 1, p.own, p.total), BF16),
            pltpu.VMEM((groups - 1, p.own, p.total), BF16),
            pltpu.VMEM((p.own, p.total), F32),
            pltpu.VMEM((p.chunks, width, p.chunk), F32),
            dma((DEPTH,)),
            dma((p.parts, n - 1)), dma((p.parts, n - 1)),
            dma((p.parts, n - 1)), dma((p.parts, n - 1)),
            dma((groups - 1,)), dma((groups - 1,)),
            dma((sends,)), dma((sends,)),
            dma((p.chunks,)), dma((p.chunks,)),
        ],
        compiler_params=pltpu.CompilerParams(
            collective_id=0, has_side_effects=True, vmem_limit_bytes=60 << 20
        ),
    )(genotypes, allele_freq[None, :], snp_bins[None, :], probes, lane_vars, noise_var)


def solution(mesh):
    placed = (P("samp", "snp"), P("snp"), P("snp"), P(None, "samp"), P())
    return jax.shard_map(
        body,
        mesh=mesh,
        in_specs=placed,
        out_specs=(P(("samp", "snp"), None), P(None, ("samp", "snp"))),
        check_vma=False,
    )
```

time: 355 us -> 114 us (0.32)
  waiting for transfers between devices: 177 us -> 0 us
  Pallas kernels: 0 us -> 103 us
  local copies, waits for them, and re-layouts: 67.9 us -> 10.5 us
  matrix products: 55.4 us -> 0 us
  other arithmetic: 29.1 us -> 0 us
  between operations: 14.1 us -> 0.65 us
  starting transfers between devices: 10.1 us -> 0 us
    pallas_call x0 -> x1, Pallas kernels: none -> 103 us  [body(): pl.pallas_call(functools.partial(kernel, p), out_shape=(jax.ShapeDtypeStr...]
    psum x1 -> x0, waiting for transfers between devices: 93.9 us -> none  [body(): lax.psum(partial_scores, 'samp') / jnp.sqrt(jnp.float32(whole_rows))]
    dot_general x3 -> x0, matrix products: 55.4 us -> none  [the longest x1 25.7 us: body(): jnp.einsum('nmb,m->bn', stacked, variances[:COMPONENTS])]
    all_to_all x1 -> x0, waiting for transfers between devices: 47.7 us -> none  [body(): lax.all_to_all(standard, 'snp', split_axis=0, concat_axis=1, tiled=True)]
    dot_general x1 -> x0, local copies, waits for them, and re-layouts: 38.3 us -> none  [body(): jnp.einsum('nmb,m->bn', stacked, variances[:COMPONENTS])]
    all_gather x1 -> x0, waiting for transfers between devices: 35.5 us -> none  [body(): gathered = lax.all_gather(packed, 'snp', axis=1, tiled=True)]
    convert_element_type x5 -> x0, other arithmetic: 23.3 us -> none  [the longest x1 18.2 us: standardize(): ((dosage_block.astype(jnp.float32) - 2.0 * allele_freq) / spread).astype(...]
    all_to_all x1 -> x0, local copies, waits for them, and re-layouts: 22.4 us -> none  [body(): lax.all_to_all(standard, 'snp', split_axis=0, concat_axis=1, tiled=True)]
  transfers between devices with their start and end apart: 3 -> 0, of which waited for: 3 -> 0; matrix products, arithmetic and copies ran while one was open for 5% -> 0% of each run, Pallas kernels for 0% -> 0%
where the time goes in v2:
time: 114 us
  Pallas kernels  103 us (90%)
  local copies, waits for them, and re-layouts  10.5 us (9%)
    pallas_call x1, Pallas kernels, body(): pl.pallas_call(functools.partial(kernel, p), out_shape=(jax.ShapeDtypeStr...  103 us
    unnamed x4, local copies, waits for them, and re-layouts  6.75 us

profile of v2, /device:TPU:0, one launch (start us, length us, event | category | flops | bytes accessed | tf_op | source)
XLA Modules:
  0.0 113.9 jit_solution(17569756618258649560)
XLA Ops:
  0.6 1.2 %slice.7 = f32[1]{0:T(128)} slice(f32[13]{0:T(128)} %param.9), slice={[12:13]} | slice | bytes 8 | tf_op jit(solution)/shard_map/slice | solution.py:277
  1.9 1.2 %broadcast_in_dim.15.noise_var = f32[1,128]{1,0:T(1,128)} broadcast(f32[]{:T(128)} %bitcast.2), dimensions={} | broadcast | bytes 516 | tf_op jit(solution)/shard_map/broadcast_in_dim | solution.py:277
  3.0 0.7 broadcast_in_dim.14
  3.7 0.7 broadcast_in_dim_reshape.3.lane_vars
  4.4 102.7 %shard_map.68 = (f32[2048,768]{1,0:T(8,128)}, f32[64,2048]{1,0:T(8,128)}) custom-call(s32[4096,2048]{1,0:T(8,128)} %geno.1, f32[1,2048]{1,0:T(1,128)} %bitcast.4, s32[1,2048]{1,0:T(1,128)} %bitcast.5, bf16[64,4096]{1,0:T(8,128)(2,1)} %probes.1, f32[1,768]{1,0:T(1,128)} %broadcast_in_dim_reshape.3.lane_vars, f32[1,128]{1,0:T(1,128)} %broadcast_in_dim.15.noise_var), custom_call_target="tpu_custom_call" | custom-call | tf_op jit(solution)/shard_map/pallas_call | solution.py:281
  107.1 0.0 copy-start
  107.1 5.9 %copy.9 = f32[2048,768]{1,0:T(8,128)} copy(f32[2048,768]{1,0:T(8,128)} %get-tuple-element.4) | data formatting | bytes 12582912
  113.1 0.0 copy-done
  113.1 0.8 copy.10
Async XLA Ops:
  107.1 6.0 %copy-start = (f32[64,2048]{1,0:T(8,128)S(1)}, f32[64,2048]{1,0:T(8,128)}, u32[]{:S(2)}) copy-start(f32[64,2048]{1,0:T(8,128)} %get-tuple-element.5) | copy-start | bytes 1572868

commit v3 on v2

--- a/solution.py
+++ b/solution.py
@@ -23,7 +23,7 @@
         self.samp, self.snp = samp, snp
         self.total = COMPONENTS * width
         self.parts = 1
-        for parts in (2,):
+        for parts in (2, 4):
             span = snps // parts
             if span % LANES == 0 and width // (samp // min(samp, span // LANES)) >= 16:
                 self.parts = parts
@@ -35,15 +35,15 @@
         self.tile = min(rows, TILE_BYTES // (4 * self.span))
         self.tiles = rows // self.tile
         self.own = rows // snp
-        self.chunk = min(256, self.own)
+        self.chunk = min(128, self.own)
         self.chunks = self.own // self.chunk
 
 
 def kernel(
-    plan, geno, freq, bins, probes, lane_vars, noise_var, out, comb,
+    plan, geno, freq, bins, probes, variances, own, comb_rows,
     dosages, standard, acc, rs_send, rs_recv, gathered, counts, factor, weights,
-    part_send, part_recv, own, comb_rows,
-    in_sem, rs_ssem, rs_rsem, ag_ssem, ag_rsem, ct_ssem, ct_rsem, ex_ssem, ex_rsem, out_sem, comb_sem,
+    part_send, part_recv,
+    in_sem, rs_ssem, rs_rsem, ag_ssem, ag_rsem, ct_ssem, ct_rsem, ex_ssem, ex_rsem,
 ):
     p = plan
     n, groups = p.samp, p.snp
@@ -188,8 +188,10 @@
     factor[...] = jnp.broadcast_to(row, factor.shape)
     for part in range(1, p.parts):
         read_part(part)
-        reduce_part(part - 1)
-    reduce_part(p.parts - 1)
+        if part >= 2:
+            reduce_part(part - 2)
+    for part in range(max(p.parts - 2, 0), p.parts):
+        reduce_part(part)
     for part in range(p.parts):
         spread_part(part)
 
@@ -219,13 +221,15 @@
         here = pl.ds(pl.multiple_of(chunk * p.chunk, p.chunk), p.chunk)
         own[here, :] = jnp.dot(standard[rows, :], weights[...], preferred_element_type=F32)
 
-    def out_copy(chunk):
-        here = pl.ds(pl.multiple_of(chunk * p.chunk, p.chunk), p.chunk)
-        return pltpu.make_async_copy(own.at[here], out.at[here], out_sem.at[chunk])
-
-    def comb_copy(chunk):
-        here = pl.ds(pl.multiple_of(chunk * p.chunk, p.chunk), p.chunk)
-        return pltpu.make_async_copy(comb_rows.at[chunk], comb.at[:, here], comb_sem.at[chunk])
+    repeat = LANES // p.width
+    lane = lax.broadcasted_iota(jnp.int32, (1, LANES), 1) // p.width
+    lane_vars = []
+    for pair in range(p.total // LANES):
+        row = jnp.full((1, LANES), variances[pair * repeat], F32)
+        for again in range(1, repeat):
+            row = jnp.where(lane == again, variances[pair * repeat + again], row)
+        lane_vars.append(row)
+    noise = variances[COMPONENTS]
 
     @pl.loop(0, p.chunks)
     def _(chunk):
@@ -235,18 +239,16 @@
             part_copy(shift * p.chunks + chunk).wait_recv()
             total = total + part_recv[shift, here, :].astype(F32)
         own[here, :] = total
-        out_copy(chunk).start()
         folded = jnp.zeros((p.chunk, LANES), F32)
         for pair in range(p.total // LANES):
             lanes = slice(pair * LANES, (pair + 1) * LANES)
-            folded = folded + total[:, lanes] * lane_vars[:, lanes]
+            folded = folded + total[:, lanes] * lane_vars[pair]
         turned = folded.T
         mixed = turned[0 : p.width]
         for again in range(1, LANES // p.width):
             mixed = mixed + turned[again * p.width : (again + 1) * p.width]
         cols = pl.ds(pl.multiple_of(mine * p.own + chunk * p.chunk, p.chunk), p.chunk)
-        comb_rows[chunk] = mixed + noise_var[:, 0:1] * probes[:, cols].astype(F32)
-        comb_copy(chunk).start()
+        comb_rows[:, here] = mixed + noise * probes[:, cols].astype(F32)
 
     @pl.loop(0, sends)
     def _(index):
@@ -261,11 +263,6 @@
 
     for shift in range(1, groups):
         count_copy(shift).wait_send()
-
-    @pl.loop(0, p.chunks)
-    def _(chunk):
-        out_copy(chunk).wait()
-        comb_copy(chunk).wait()
 
 
 def body(genotypes, allele_freq, snp_bins, probes, variances):
@@ -273,19 +270,17 @@
     width = probes.shape[0]
     p = Plan(rows, snps, width, lax.axis_size("samp"), lax.axis_size("snp"))
     n, groups = p.samp, p.snp
-    lane_vars = jnp.repeat(variances[:COMPONENTS], width)[None, :]
-    noise_var = jnp.broadcast_to(variances[COMPONENTS], (1, LANES))
     vmem, hbm = pl.BlockSpec(memory_space=pltpu.VMEM), pl.BlockSpec(memory_space=pl.ANY)
     dma = pltpu.SemaphoreType.DMA
     sends = (groups - 1) * p.chunks
     return pl.pallas_call(
         functools.partial(kernel, p),
         out_shape=(
-            jax.ShapeDtypeStruct((p.own, p.total), F32),
-            jax.ShapeDtypeStruct((width, p.own), F32),
+            pltpu.VMEM((p.own, p.total), F32),
+            pltpu.VMEM((width, p.own), F32),
         ),
-        in_specs=[hbm, vmem, vmem, vmem, vmem, vmem],
-        out_specs=(hbm, hbm),
+        in_specs=[hbm, vmem, vmem, vmem, pl.BlockSpec(memory_space=pltpu.SMEM)],
+        out_specs=(vmem, vmem),
         scratch_shapes=[
             pltpu.VMEM((DEPTH, p.tile, p.span), jnp.int32),
             pltpu.VMEM((rows, snps), BF16),
@@ -298,19 +293,16 @@
             pltpu.VMEM((snps, p.total), BF16),
             pltpu.VMEM((groups - 1, p.own, p.total), BF16),
             pltpu.VMEM((groups - 1, p.own, p.total), BF16),
-            pltpu.VMEM((p.own, p.total), F32),
-            pltpu.VMEM((p.chunks, width, p.chunk), F32),
             dma((DEPTH,)),
             dma((p.parts, n - 1)), dma((p.parts, n - 1)),
             dma((p.parts, n - 1)), dma((p.parts, n - 1)),
             dma((groups - 1,)), dma((groups - 1,)),
             dma((sends,)), dma((sends,)),
-            dma((p.chunks,)), dma((p.chunks,)),
         ],
         compiler_params=pltpu.CompilerParams(
-            collective_id=0, has_side_effects=True, vmem_limit_bytes=60 << 20
+            collective_id=0, has_side_effects=True, vmem_limit_bytes=44 << 20
         ),
-    )(genotypes, allele_freq[None, :], snp_bins[None, :], probes, lane_vars, noise_var)
+    )(genotypes, allele_freq[None, :], snp_bins[None, :], probes, variances)
 
 
 def solution(mesh):

time: 114 us -> 109 us (0.956)
  local copies, waits for them, and re-layouts: 10.5 us -> 6.58 us
    broadcast_in_dim x2 -> x0, local copies, waits for them, and re-layouts: 1.88 us -> none  [the longest x1 1.16 us: body(): noise_var = jnp.broadcast_to(variances[COMPONENTS], (1, LANES))]
    slice x1 -> x0, local copies, waits for them, and re-layouts: 1.24 us -> none  [body(): noise_var = jnp.broadcast_to(variances[COMPONENTS], (1, LANES))]
    unnamed x4 -> x10, local copies, waits for them, and re-layouts: 6.75 us -> 6.58 us
where the time goes in v3:
time: 109 us
  Pallas kernels  102 us (94%)
  local copies, waits for them, and re-layouts  6.58 us (6%)
    pallas_call x1, Pallas kernels, body(): pl.pallas_call(functools.partial(kernel, p), out_shape=(pltpu.VMEM((p.own...  102 us
    unnamed x10, local copies, waits for them, and re-layouts  6.58 us

profile of v3, /device:TPU:0, one launch (start us, length us, event | category | flops | bytes accessed | tf_op | source)
XLA Modules:
  0.0 109.0 jit_solution(4166547012555333938)
XLA Ops:
  0.6 0.0 copy-start
  0.6 1.0 copy-done
  1.7 0.0 copy-start.1
  1.7 0.7 copy-done.1
  2.4 0.0 copy-start.2
  2.4 0.7 copy-done.2
  3.1 0.0 copy-start.3
  3.1 0.7 copy-done.3
  3.7 101.8 %shard_map.68 = (f32[2048,768]{1,0:T(8,128)S(1)}, f32[64,2048]{1,0:T(8,128)S(1)}) custom-call(s32[4096,2048]{1,0:T(8,128)} %geno.1, f32[1,2048]{1,0:T(1,128)S(1)} %bitcast.2, s32[1,2048]{1,0:T(1,128)S(1)} %bitcast.3, bf16[64,4096]{1,0:T(8,128)(2,1)S(1)} %copy-done, f32[13]{0:T(128)S(1)} %copy-done.3), custom_call_target="tpu_custom_call" | custom-call | tf_op jit(solution)/shard_map/pallas_call | solution.py:276
  105.5 2.7 %copy.9 = f32[2048,768]{1,0:T(8,128)} copy(f32[2048,768]{1,0:T(8,128)S(1)} %get-tuple-element.2) | data formatting | bytes 12582912
  108.2 0.8 copy.10
Async XLA Ops:
  0.6 1.0 copy-start
  1.7 0.7 copy-start.1
  2.4 0.7 copy-start.2
  3.1 0.7 copy-start.3

commit v4 on v3

--- a/solution.py
+++ b/solution.py
@@ -11,7 +11,8 @@
 LABELS = 16
 LANES = 128
 TILE_BYTES = 2 << 20
-DEPTH = 3
+DEPTH = 8
+VMEM_BYTES = 67_043_328
 MESH = pl.DeviceIdType.MESH
 F32 = jnp.float32
 BF16 = jnp.bfloat16
@@ -40,10 +41,11 @@
 
 
 def kernel(
-    plan, geno, freq, bins, probes, variances, own, comb_rows,
+    plan, geno, freq_in, bins_in, probes_in, variances, own, comb_rows,
+    freq, bins, probes,
     dosages, standard, acc, rs_send, rs_recv, gathered, counts, factor, weights,
     part_send, part_recv,
-    in_sem, rs_ssem, rs_rsem, ag_ssem, ag_rsem, ct_ssem, ct_rsem, ex_ssem, ex_rsem,
+    small_sem, in_sem, rs_ssem, rs_rsem, ag_ssem, ag_rsem, ct_ssem, ct_rsem, ex_ssem, ex_rsem,
 ):
     p = plan
     n, groups = p.samp, p.snp
@@ -57,6 +59,13 @@
             in_sem.at[slot],
         )
 
+    small = [
+        pltpu.make_async_copy(source, held, small_sem.at[place])
+        for place, (source, held) in enumerate(((bins_in, bins), (freq_in, freq), (probes_in, probes)))
+    ]
+    for copy in small:
+        copy.start()
+
     steps = p.parts * p.tiles
     for step in range(min(DEPTH - 1, steps)):
         fetch(step).start()
@@ -75,6 +84,8 @@
             barrier, inc=1, device_id={"samp": me, "snp": (mine + shift) % groups}, device_id_type=MESH
         )
 
+    for copy in small:
+        copy.wait()
     labels = lax.broadcasted_iota(jnp.int32, (LABELS, p.snps), 0)
     hits = labels == bins[...]
     counted = jnp.sum(hits.astype(F32), axis=1, keepdims=True)
@@ -271,6 +282,7 @@
     p = Plan(rows, snps, width, lax.axis_size("samp"), lax.axis_size("snp"))
     n, groups = p.samp, p.snp
     vmem, hbm = pl.BlockSpec(memory_space=pltpu.VMEM), pl.BlockSpec(memory_space=pl.ANY)
+    held = pl.BlockSpec(memory_space=pltpu.HBM)
     dma = pltpu.SemaphoreType.DMA
     sends = (groups - 1) * p.chunks
     return pl.pallas_call(
@@ -279,9 +291,12 @@
             pltpu.VMEM((p.own, p.total), F32),
             pltpu.VMEM((width, p.own), F32),
         ),
-        in_specs=[hbm, vmem, vmem, vmem, pl.BlockSpec(memory_space=pltpu.SMEM)],
+        in_specs=[hbm, held, held, held, pl.BlockSpec(memory_space=pltpu.SMEM)],
         out_specs=(vmem, vmem),
         scratch_shapes=[
+            pltpu.VMEM((1, snps), F32),
+            pltpu.VMEM((1, snps), jnp.int32),
+            pltpu.VMEM((width, rows), BF16),
             pltpu.VMEM((DEPTH, p.tile, p.span), jnp.int32),
             pltpu.VMEM((rows, snps), BF16),
             pltpu.VMEM((width, snps), F32),
@@ -293,6 +308,7 @@
             pltpu.VMEM((snps, p.total), BF16),
             pltpu.VMEM((groups - 1, p.own, p.total), BF16),
             pltpu.VMEM((groups - 1, p.own, p.total), BF16),
+            dma((3,)),
             dma((DEPTH,)),
             dma((p.parts, n - 1)), dma((p.parts, n - 1)),
             dma((p.parts, n - 1)), dma((p.parts, n - 1)),
@@ -300,7 +316,7 @@
             dma((sends,)), dma((sends,)),
         ],
         compiler_params=pltpu.CompilerParams(
-            collective_id=0, has_side_effects=True, vmem_limit_bytes=44 << 20
+            collective_id=0, has_side_effects=True, vmem_limit_bytes=VMEM_BYTES - 4 * p.own * (p.total + width) - 8192
         ),
     )(genotypes, allele_freq[None, :], snp_bins[None, :], probes, variances)
 

time: 109 us -> 104 us (0.954)
  local copies, waits for them, and re-layouts: 6.58 us -> 3.5 us
  Pallas kernels: 102 us -> 99.9 us
    unnamed x10 -> x2, local copies, waits for them, and re-layouts: 6.58 us -> 3.5 us
    pallas_call x1, Pallas kernels: 102 us -> 99.9 us  [body(): pl.pallas_call(functools.partial(kernel, p), out_shape=(pltpu.VMEM((p.own...]
where the time goes in v4:
time: 104 us
  Pallas kernels  99.9 us (96%)
  local copies, waits for them, and re-layouts  3.5 us (3%)
    pallas_call x1, Pallas kernels, body(): pl.pallas_call(functools.partial(kernel, p), out_shape=(pltpu.VMEM((p.own...  99.9 us
    unnamed x2, local copies, waits for them, and re-layouts  3.5 us

profile of v4, /device:TPU:0, one launch (start us, length us, event | category | flops | bytes accessed | tf_op | source)
XLA Modules:
  0.0 104.1 jit_solution(12733346504468610051)
XLA Ops:
  0.6 99.9 %shard_map.68 = (f32[2048,768]{1,0:T(8,128)S(1)}, f32[64,2048]{1,0:T(8,128)S(1)}) custom-call(s32[4096,2048]{1,0:T(8,128)} %geno.1, f32[1,2048]{1,0:T(1,128)} %bitcast.2, s32[1,2048]{1,0:T(1,128)} %bitcast.3, bf16[64,4096]{1,0:T(8,128)(2,1)} %probes_in.1, f32[13]{0:T(128)} %variances.1), custom_call_target="tpu_custom_call" | custom-call | tf_op jit(solution)/shard_map/pallas_call | solution.py:288
  100.6 2.7 %copy.9 = f32[2048,768]{1,0:T(8,128)} copy(f32[2048,768]{1,0:T(8,128)S(1)} %get-tuple-element.2) | data formatting | bytes 12582912
  103.3 0.8 copy.10

commit v5 on v4

--- a/solution.py
+++ b/solution.py
@@ -10,8 +10,8 @@
 COMPONENTS = 12
 LABELS = 16
 LANES = 128
-TILE_BYTES = 2 << 20
-DEPTH = 8
+TILE_BYTES = 4 << 20
+DEPTH = 5
 VMEM_BYTES = 67_043_328
 MESH = pl.DeviceIdType.MESH
 F32 = jnp.float32
@@ -201,9 +201,13 @@
         read_part(part)
         if part >= 2:
             reduce_part(part - 2)
-    for part in range(max(p.parts - 2, 0), p.parts):
+    early = max(p.parts - 2, 0)
+    for part in range(early, p.parts - 1):
         reduce_part(part)
-    for part in range(p.parts):
+    for part in range(early):
+        spread_part(part)
+    reduce_part(p.parts - 1)
+    for part in range(early, p.parts):
         spread_part(part)
 
     def part_copy(index):

time: 104 us -> 105 us (level)
  Pallas kernels: 99.9 us -> 101 us
where the time goes in v5:
time: 105 us
  Pallas kernels  101 us (96%)
  local copies, waits for them, and re-layouts  3.5 us (3%)
    pallas_call x1, Pallas kernels, body(): pl.pallas_call(functools.partial(kernel, p), out_shape=(pltpu.VMEM((p.own...  101 us
    unnamed x2, local copies, waits for them, and re-layouts  3.5 us

profile of v5, /device:TPU:0, one launch (start us, length us, event | category | flops | bytes accessed | tf_op | source)
XLA Modules:
  0.0 104.7 jit_solution(11985213061582805974)
XLA Ops:
  0.6 100.6 %shard_map.68 = (f32[2048,768]{1,0:T(8,128)S(1)}, f32[64,2048]{1,0:T(8,128)S(1)}) custom-call(s32[4096,2048]{1,0:T(8,128)} %geno.1, f32[1,2048]{1,0:T(1,128)} %bitcast.2, s32[1,2048]{1,0:T(1,128)} %bitcast.3, bf16[64,4096]{1,0:T(8,128)(2,1)} %probes_in.1, f32[13]{0:T(128)} %variances.1), custom_call_target="tpu_custom_call" | custom-call | tf_op jit(solution)/shard_map/pallas_call | solution.py:292
  101.2 2.7 %copy.9 = f32[2048,768]{1,0:T(8,128)} copy(f32[2048,768]{1,0:T(8,128)S(1)} %get-tuple-element.2) | data formatting | bytes 12582912
  103.9 0.8 copy.10
